TPU v7x, 128 devices: a whole 4x4x4 slice. The times are simulated.
128 devices in a mesh: row: 8 (over z, core), col: 16 (over y, x).
Axes of the slice: x: 4, y: 4, z: 4, core: 2. Of those that a mesh axis runs over, the one named last changes fastest.
Arguments:
- inputs: bfloat16 [512, 8192], P('row', 'col'), may hold values from -6 to 6
- grad_out: bfloat16 [512, 8192], P('row', 'col'), may hold values from -0.1796875 to 0.1796875
- gate_pre: bfloat16 [512, 28672], P('col', 'row'), may hold values from -6 to 6
- up_pre: bfloat16 [512, 28672], P('col', 'row'), may hold values from -6 to 6
- w_gate: bfloat16 [8192, 28672], P('col', 'row'), may hold values from -0.25 to 0.25
- w_up: bfloat16 [8192, 28672], P('col', 'row'), may hold values from -0.25 to 0.25
- w_down: bfloat16 [28672, 8192], P('row', 'col'), may hold values from -0.03125 to 0.03125
Outputs:
- grad_inputs: bfloat16 [512, 8192], P('row', 'col')
- grad_gate: bfloat16 [8192, 28672], P('col', 'row')
- grad_up: bfloat16 [8192, 28672], P('col', 'row')
- grad_down: bfloat16 [28672, 8192], P('row', 'col')
All inputs are finite; a program needn't handle non-finite values.
Results may differ from a plain program's by a relative error of at most 0.005.
Values may be sent and summed in bfloat16 or wider, within the bound.
A program may use at most 128 MiB of HBM per device.

v0:
```python
import jax
import jax.numpy as jnp
from jax import lax
from jax.sharding import PartitionSpec as P


def swiglu_back(gate_pre, up_pre, hidden_grad):
    gate_wide = gate_pre.astype(jnp.float32)
    up_wide = up_pre.astype(jnp.float32)
    logistic = jax.nn.sigmoid(gate_wide)
    swished = gate_wide * logistic
    hidden = (swished * up_wide).astype(jnp.bfloat16)
    up_grad = (hidden_grad * swished).astype(jnp.bfloat16)
    gate_grad = (hidden_grad * up_wide * logistic * (1.0 + gate_wide * (1.0 - logistic))).astype(
        jnp.bfloat16
    )
    return (hidden, gate_grad, up_grad)


def on_device(inputs, grad_out, gate_pre, up_pre, w_gate, w_up, w_down):
    last_last = (((1,), (1,)), ((), ()))
    first_first = (((0,), (0,)), ((), ()))
    inputs_all, grad_out_all = (
        lax.all_gather(inputs, "row", axis=0, tiled=True),
        lax.all_gather(grad_out, "row", axis=0, tiled=True),
    )
    hidden_grad = lax.psum_scatter(
        lax.dot_general(grad_out_all, w_down, last_last, preferred_element_type=jnp.float32),
        "col",
        scatter_dimension=0,
        tiled=True,
    )
    hidden, gate_grad, up_grad = swiglu_back(gate_pre, up_pre, hidden_grad)
    hidden_all, gate_grad_all, up_grad_all = (
        lax.all_gather(hidden, "col", axis=0, tiled=True),
        lax.all_gather(gate_grad, "col", axis=0, tiled=True),
        lax.all_gather(up_grad, "col", axis=0, tiled=True),
    )
    grad_down = lax.dot_general(
        hidden_all, grad_out_all, first_first, preferred_element_type=jnp.float32
    ).astype(jnp.bfloat16)
    grad_gate = lax.dot_general(
        inputs_all, gate_grad_all, first_first, preferred_element_type=jnp.float32
    ).astype(jnp.bfloat16)
    grad_up = lax.dot_general(
        inputs_all, up_grad_all, first_first, preferred_element_type=jnp.float32
    ).astype(jnp.bfloat16)
    summed = lax.dot_general(gate_grad_all, w_gate, last_last, preferred_element_type=jnp.float32)
    grad_inputs = lax.psum_scatter(
        summed + lax.dot_general(up_grad_all, w_up, last_last, preferred_element_type=jnp.float32),
        "row",
        scatter_dimension=0,
        tiled=True,
    ).astype(jnp.bfloat16)
    return (grad_inputs, grad_gate, grad_up, grad_down)


def solution(mesh):
    placed = (
        P("row", "col"),
        P("row", "col"),
        P("col", "row"),
        P("col", "row"),
        P("col", "row"),
        P("col", "row"),
        P("row", "col"),
    )
    return jax.shard_map(
        on_device,
        mesh=mesh,
        in_specs=placed,
        out_specs=(P("row", "col"), P("col", "row"), P("col", "row"), P("row", "col")),
        check_vma=False,
    )
```

profile of v0, /device:TPU:0, one launch (start us, length us, event | category | flops | bytes accessed | tf_op | source)
XLA Modules:
  0.0 309.3 jit_solution(8646618759056539256)
XLA Ops:
  7.2 0.0 reduce-scatter.3.cloned.1.call-start
  7.2 14.6 %all_gather.15 = bf16[512,512]{1,0:T(8,128)(2,1)S(1)} all-gather(bf16[64,512]{1,0:T(8,128)(2,1)} %param.8), channel_id=1, replica_groups=mesh['row'=8,'col'=16] {'row'}, dimensions={0}, use_global_device_ids=true | all-gather | bytes 589824 | tf_op jit(solution)/shard_map/all_gather | solution.py:25
  21.8 7.1 %fusion.10 = f32[512,3584]{1,0:T(8,128)} fusion(bf16[512,512]{1,0:T(8,128)(2,1)S(1)} %all_gather.15, bf16[3584,512]{1,0:T(8,128)(2,1)} %param.13), kind=kOutput, calls=%fused_computation.20 | convolution fusion | flops 1879048192 | bytes 11534336 | tf_op jit(solution)/shard_map/dot_general | solution.py:28
  28.9 0.0 copy-start
  28.9 0.0 copy-start.1
  28.9 0.0 reduce-scatter.3.cloned.1.call-update
  28.9 0.0 all-gather.4.cloned.1.call-start
  29.0 84.0 %reduce-scatter.3.cloned.1.call-done = f32[32,3584]{1,0:T(8,128)} async-done(((f32[512,3584]{1,0:T(8,128)}), f32[32,3584]{1,0:T(8,128)}) %reduce-scatter.3.cloned.1.call-update) | async-done | bytes 458768 | tf_op jit(solution)/shard_map/reduce_scatter | solution.py:27
  113.0 0.0 copy-done
  113.0 0.0 copy-done.1
  113.0 2.1 multiply_convert_fusion
  115.1 0.0 all-gather.4.cloned.1.call-update
  115.1 0.0 all-gather.6.cloned.1.call-start
  115.2 0.7 all-gather.6.cloned.1.call-update
  115.9 0.0 all-gather.8.cloned.1.call-start
  115.9 0.5 all-gather.8.cloned.1.call-update
  116.4 0.0 reduce-scatter.5.cloned.1.call-start
  116.5 48.4 %all-gather.4.cloned.1.call-done = bf16[512,3584]{1,0:T(8,128)(2,1)} async-done(((bf16[32,3584]{1,0:T(8,128)(2,1)}), bf16[512,3584]{1,0:T(8,128)(2,1)}) %all-gather.4.cloned.1.call-update) | async-done | bytes 3670032 | tf_op jit(solution)/shard_map/all_gather | solution.py:36
  164.9 5.2 %fusion.11 = f32[512,512]{1,0:T(8,128)S(1)} fusion(bf16[512,3584]{1,0:T(8,128)(2,1)} %all-gather.4.cloned.1.call-done, bf16[512,3584]{1,0:T(8,128)(2,1)} %param.11), kind=kOutput, calls=%fused_computation.21 | convolution fusion | flops 1879048192 | bytes 8388608 | tf_op jit(solution)/shard_map/dot_general | solution.py:48
  170.1 0.0 copy-start.2
  170.1 46.5 %all-gather.6.cloned.1.call-done = bf16[512,3584]{1,0:T(8,128)(2,1)} async-done(((bf16[32,3584]{1,0:T(8,128)(2,1)}), bf16[512,3584]{1,0:T(8,128)(2,1)}) %all-gather.6.cloned.1.call-update) | async-done | bytes 3670032 | tf_op jit(solution)/shard_map/all_gather | solution.py:37
  216.6 6.2 %convolution_add_fusion = f32[512,512]{1,0:T(8,128)} fusion(f32[512,512]{1,0:T(8,128)S(1)} %fusion.11, bf16[512,3584]{1,0:T(8,128)(2,1)} %all-gather.6.cloned.1.call-done, bf16[512,3584]{1,0:T(8,128)(2,1)} %param.12), kind=kOutput, calls=%fused_computation.5 | convolution fusion | flops 1879310336 | bytes 9437184 | tf_op jit(solution)/shard_map/dot_general | solution.py:50
  222.8 0.0 reduce-scatter.5.cloned.1.call-update
  222.8 0.0 copy-done.2
  222.8 13.8 %all_gather.18 = bf16[512,512]{1,0:T(8,128)(2,1)S(1)} all-gather(bf16[64,512]{1,0:T(8,128)(2,1)S(1)} %copy-done.2), channel_id=1, replica_groups=mesh['row'=8,'col'=16] {'row'}, dimensions={0}, use_global_device_ids=true | all-gather | bytes 589824 | tf_op jit(solution)/shard_map/all_gather | solution.py:24
  236.6 6.0 %fusion = bf16[512,3584]{0,1:T(8,128)(2,1)} fusion(bf16[512,3584]{1,0:T(8,128)(2,1)} %all-gather.4.cloned.1.call-done, bf16[512,512]{1,0:T(8,128)(2,1)S(1)} %all_gather.18), kind=kOutput, calls=%fused_computation.3 | convolution fusion | flops 1880883200 | bytes 7864320 | tf_op jit(solution)/shard_map/dot_general | solution.py:42
  242.6 5.9 %copy.11 = bf16[512,3584]{1,0:T(8,128)(2,1)} copy(bf16[512,3584]{0,1:T(8,128)(2,1)} %fusion) | data formatting | bytes 7340032
  248.5 6.0 %fusion.1 = bf16[512,3584]{0,1:T(8,128)(2,1)} fusion(bf16[512,3584]{1,0:T(8,128)(2,1)} %all-gather.6.cloned.1.call-done, bf16[512,512]{1,0:T(8,128)(2,1)S(1)} %all_gather.18), kind=kOutput, calls=%fused_computation.4 | convolution fusion | flops 1880883200 | bytes 7864320 | tf_op jit(solution)/shard_map/dot_general | solution.py:45
  254.5 5.9 %copy.12 = bf16[512,3584]{1,0:T(8,128)(2,1)} copy(bf16[512,3584]{0,1:T(8,128)(2,1)} %fusion.1) | data formatting | bytes 7340032
  260.5 7.1 %all-gather.8.cloned.1.call-done = bf16[512,3584]{1,0:T(8,128)(2,1)} async-done(((bf16[32,3584]{1,0:T(8,128)(2,1)}), bf16[512,3584]{1,0:T(8,128)(2,1)}) %all-gather.8.cloned.1.call-update) | async-done | bytes 3670032 | tf_op jit(solution)/shard_map/all_gather | solution.py:35
  267.6 6.0 %convolution_convert_fusion = bf16[3584,512]{1,0:T(8,128)(2,1)} fusion(bf16[512,3584]{1,0:T(8,128)(2,1)} %all-gather.8.cloned.1.call-done, bf16[512,512]{1,0:T(8,128)(2,1)S(1)} %all_gather.15), kind=kOutput, calls=%fused_computation | convolution fusion | flops 1880883200 | bytes 7864320 | tf_op jit(solution)/shard_map/dot_general | solution.py:39
  273.6 27.6 %reduce-scatter.5.cloned.1.call-done = f32[64,512]{1,0:T(8,128)} async-done(((f32[512,512]{1,0:T(8,128)}), f32[64,512]{1,0:T(8,128)}) %reduce-scatter.5.cloned.1.call-update) | async-done | bytes 131088 | tf_op jit(solution)/shard_map/reduce_scatter | solution.py:49
  301.2 1.5 convert_element_type.37
Async XLA Ops:
  7.2 105.8 %reduce-scatter.3.cloned.1.call-start = ((), (), s32[]{:S(2)}) async-start(), calls=%async_computation.2 | async-start | bytes 7798784 | tf_op jit(solution)/shard_map/reduce_scatter | solution.py:27
  28.9 84.1 %copy-start = (bf16[32,3584]{1,0:T(8,128)(2,1)S(1)}, bf16[32,3584]{1,0:T(8,128)(2,1)}, u32[]{:S(2)}) copy-start(bf16[32,3584]{1,0:T(8,128)(2,1)} %param.9) | copy-start | bytes 688132
  28.9 84.1 %copy-start.1 = (bf16[32,3584]{1,0:T(8,128)(2,1)S(1)}, bf16[32,3584]{1,0:T(8,128)(2,1)}, u32[]{:S(2)}) copy-start(bf16[32,3584]{1,0:T(8,128)(2,1)} %param.10) | copy-start | bytes 688132
  28.9 135.9 %all-gather.4.cloned.1.call-start = ((), (), s32[]{:S(2)}) async-start(), calls=%async_computation.3 | async-start | bytes 3899392 | tf_op jit(solution)/shard_map/all_gather | solution.py:36
  115.1 101.5 %all-gather.6.cloned.1.call-start = ((), (), s32[]{:S(2)}) async-start(), calls=%async_computation.4 | async-start | bytes 3899392 | tf_op jit(solution)/shard_map/all_gather | solution.py:37
  115.9 151.7 %all-gather.8.cloned.1.call-start = ((), (), s32[]{:S(2)}) async-start(), calls=%async_computation.6 | async-start | bytes 3899392 | tf_op jit(solution)/shard_map/all_gather | solution.py:35
  116.4 184.8 %reduce-scatter.5.cloned.1.call-start = ((), (), s32[]{:S(2)}) async-start(), calls=%async_computation.5 | async-start | bytes 1179648 | tf_op jit(solution)/shard_map/reduce_scatter | solution.py:49
  170.1 52.7 %copy-start.2 = (bf16[64,512]{1,0:T(8,128)(2,1)S(1)}, bf16[64,512]{1,0:T(8,128)(2,1)}, u32[]{:S(2)}) copy-start(bf16[64,512]{1,0:T(8,128)(2,1)} %param.7) | copy-start | bytes 196612
Sparse Core Ops, SparseCore 0:
  29.0 83.9 reduce-scatter.2
  115.9 48.8 all-gather.3
  167.8 48.7 all-gather.5
  218.8 48.7 all-gather.7
  270.0 31.2 reduce-scatter.4
where the time goes:
time: 310 us; the launch traced here: 309 us
  waiting for transfers between devices  215 us (69%)
  matrix products  36.5 us (12%)
  blocking collectives  28.4 us (9%)
  between operations  13.8 us (4%)
  local copies, waits for them, and re-layouts  11.9 us (4%)
  other arithmetic  3.61 us (1%)
    reduce_scatter x1, waiting for transfers between devices, on_device(): lax.psum_scatter(lax.dot_general(grad_out_all, w_down, last_last, preferr...  84 us
    all_gather x1, waiting for transfers between devices, on_device(): lax.all_gather(gate_grad, 'col', axis=0, tiled=True)  48.4 us
    all_gather x1, waiting for transfers between devices, on_device(): lax.all_gather(up_grad, 'col', axis=0, tiled=True)  46.5 us
    reduce_scatter x1, waiting for transfers between devices, on_device(): lax.psum_scatter(summed + lax.dot_general(up_grad_all, w_up, last_last, p...  27.6 us
    all_gather x1, blocking collectives, on_device(): lax.all_gather(grad_out, 'row', axis=0, tiled=True)  14.6 us
    all_gather x1, blocking collectives, on_device(): lax.all_gather(inputs, 'row', axis=0, tiled=True)  13.8 us
    unnamed x8, local copies, waits for them, and re-layouts  11.9 us
    all_gather x1, waiting for transfers between devices, on_device(): lax.all_gather(hidden, 'col', axis=0, tiled=True)  7.13 us
  transfers between devices with their start and end apart: 5, of which 5 were waited for; matrix products, arithmetic and copies ran while one was open for 13% of the time, Pallas kernels for 0%

commit v1 on v0

--- a/solution.py
+++ b/solution.py
@@ -2,6 +2,16 @@
 import jax.numpy as jnp
 from jax import lax
 from jax.sharding import PartitionSpec as P
+
+finish_files = lambda vector: jnp.concatenate(
+    lax.all_to_all(
+        jnp.stack([vector for _ in range(lax.axis_size("col"))]),
+        axis_name="col",
+        split_axis=0,
+        concat_axis=0,
+    ),
+    axis=0,
+)
 
 
 def swiglu_back(gate_pre, up_pre, hidden_grad):
@@ -33,7 +43,7 @@
     hidden, gate_grad, up_grad = swiglu_back(gate_pre, up_pre, hidden_grad)
     hidden_all, gate_grad_all, up_grad_all = (
         lax.all_gather(hidden, "col", axis=0, tiled=True),
-        lax.all_gather(gate_grad, "col", axis=0, tiled=True),
+        finish_files(gate_grad),
         lax.all_gather(up_grad, "col", axis=0, tiled=True),
     )
     grad_down = lax.dot_general(

time: 310 us -> 282 us (0.910)
  waiting for transfers between devices: 215 us -> 134 us
  blocking collectives: 28.4 us -> 82.1 us
    all_to_all x0 -> x1, blocking collectives: none -> 53.7 us  [lax.all_to_all(jnp.stack([vector for _ in range(lax.axis_size('col'))]),...]
    all_gather x1 -> x0, waiting for transfers between devices: 48.4 us -> none  [on_device(): lax.all_gather(gate_grad, 'col', axis=0, tiled=True)]
    all_gather x1, waiting for transfers between devices: 46.5 us -> 14.2 us  [on_device(): lax.all_gather(up_grad, 'col', axis=0, tiled=True)]
    dot_general x1, matrix products: 5.24 us -> 2.08 us  [on_device(): lax.dot_general(gate_grad_all, w_gate, last_last, preferred_element_type=...]
    unnamed x8 -> x12, local copies, waits for them, and re-layouts: 11.9 us -> 13.7 us
  transfers between devices with their start and end apart: 5 -> 4, of which waited for: 5 -> 4; matrix products, arithmetic and copies ran while one was open for 13% -> 14% of each run, Pallas kernels for 0% -> 0%
where the time goes in v1:
time: 282 us; the launch traced here: 281 us
  waiting for transfers between devices  134 us (48%)
  blocking collectives  82.1 us (29%)
  matrix products  33.5 us (12%)
  local copies, waits for them, and re-layouts  14 us (5%)
  between operations  13.8 us (5%)
  other arithmetic  3.61 us (1%)
    reduce_scatter x1, waiting for transfers between devices, on_device(): lax.psum_scatter(lax.dot_general(grad_out_all, w_down, last_last, preferr...  84.3 us
    all_to_all x1, blocking collectives, lax.all_to_all(jnp.stack([vector for _ in range(lax.axis_size('col'))]),...  53.7 us
    reduce_scatter x1, waiting for transfers between devices, on_device(): lax.psum_scatter(summed + lax.dot_general(up_grad_all, w_up, last_last, p...  27.7 us
    all_gather x1, blocking collectives, on_device(): lax.all_gather(grad_out, 'row', axis=0, tiled=True)  14.6 us
    all_gather x1, waiting for transfers between devices, on_device(): lax.all_gather(up_grad, 'col', axis=0, tiled=True)  14.2 us
    all_gather x1, blocking collectives, on_device(): lax.all_gather(inputs, 'row', axis=0, tiled=True)  13.8 us
    unnamed x12, local copies, waits for them, and re-layouts  13.7 us
    all_gather x1, waiting for transfers between devices, on_device(): lax.all_gather(hidden, 'col', axis=0, tiled=True)  7.18 us
  transfers between devices with their start and end apart: 4, of which 4 were waited for; matrix products, arithmetic and copies ran while one was open for 14% of the time, Pallas kernels for 0%

profile of v1, /device:TPU:0, one launch (start us, length us, event | category | flops | bytes accessed | tf_op | source)
XLA Modules:
  0.0 281.4 jit_solution(453135593003724417)
XLA Ops:
  7.2 0.0 reduce-scatter.3.cloned.1.call-start
  7.2 14.6 %all_gather.12 = bf16[512,512]{1,0:T(8,128)(2,1)S(1)} all-gather(bf16[64,512]{1,0:T(8,128)(2,1)} %param.8), channel_id=1, replica_groups=mesh['row'=8,'col'=16] {'row'}, dimensions={0}, use_global_device_ids=true | all-gather | bytes 589824 | tf_op jit(solution)/shard_map/all_gather | solution.py:35
  21.8 7.1 %fusion.10 = f32[512,3584]{1,0:T(8,128)} fusion(bf16[512,512]{1,0:T(8,128)(2,1)S(1)} %all_gather.12, bf16[3584,512]{1,0:T(8,128)(2,1)} %param.13), kind=kOutput, calls=%fused_computation.20 | convolution fusion | flops 1879048192 | bytes 11534336 | tf_op jit(solution)/shard_map/dot_general | solution.py:38
  28.9 0.0 copy-start.1
  28.9 0.0 copy-start.2
  28.9 0.0 reduce-scatter.3.cloned.1.call-update
  28.9 0.0 all-gather.3.cloned.1.call-start
  29.0 84.3 %reduce-scatter.3.cloned.1.call-done = f32[32,3584]{1,0:T(8,128)} async-done(((f32[512,3584]{1,0:T(8,128)}), f32[32,3584]{1,0:T(8,128)}) %reduce-scatter.3.cloned.1.call-update) | async-done | bytes 458768 | tf_op jit(solution)/shard_map/reduce_scatter | solution.py:37
  113.3 0.0 copy-done.1
  113.3 0.0 copy-done.2
  113.3 2.1 multiply_convert_fusion
  115.4 0.0 all-gather.3.cloned.1.call-update
  115.4 0.0 all-gather.5.cloned.1.call-start
  115.4 0.7 all-gather.5.cloned.1.call-update
  116.1 0.0 reduce-scatter.5.cloned.1.call-start
  116.2 0.3 stack.2
  116.5 0.0 copy-start.4
  116.5 53.7 %all_to_all.5 = bf16[16,32,3584]{2,1,0:T(8,128)(2,1)S(1)} all-to-all(bf16[16,32,3584]{2,1,0:T(8,128)(2,1)S(1)} %stack.2), channel_id=1, replica_groups=mesh['row'=8,'col'=16] {'col'}, dimensions={0} | all-to-all | bytes 7340032 | tf_op jit(solution)/shard_map/all_to_all | solution.py:7
  170.3 0.0 copy-start
  170.3 1.8 copy-done
  172.1 0.0 copy-done.4
  172.1 2.1 fusion.11
  174.2 0.0 copy-start.3
  174.2 14.2 %all-gather.3.cloned.1.call-done = bf16[512,3584]{1,0:T(8,128)(2,1)} async-done(((bf16[32,3584]{1,0:T(8,128)(2,1)}), bf16[512,3584]{1,0:T(8,128)(2,1)}) %all-gather.3.cloned.1.call-update) | async-done | bytes 3670032 | tf_op jit(solution)/shard_map/all_gather | solution.py:47
  188.5 6.3 %convolution_add_fusion = f32[512,512]{1,0:T(8,128)} fusion(f32[512,512]{1,0:T(8,128)S(1)} %fusion.11, bf16[512,3584]{1,0:T(8,128)(2,1)} %all-gather.3.cloned.1.call-done, bf16[512,3584]{1,0:T(8,128)(2,1)} %param.12), kind=kOutput, calls=%fused_computation.5 | convolution fusion | flops 1879310336 | bytes 9437184 | tf_op jit(solution)/shard_map/dot_general | solution.py:60
  194.7 0.0 reduce-scatter.5.cloned.1.call-update
  194.8 0.0 copy-done.3
  194.8 13.8 %all_gather.14 = bf16[512,512]{1,0:T(8,128)(2,1)S(1)} all-gather(bf16[64,512]{1,0:T(8,128)(2,1)S(1)} %copy-done.3), channel_id=1, replica_groups=mesh['row'=8,'col'=16] {'row'}, dimensions={0}, use_global_device_ids=true | all-gather | bytes 589824 | tf_op jit(solution)/shard_map/all_gather | solution.py:34
  208.5 6.0 %fusion = bf16[512,3584]{0,1:T(8,128)(2,1)} fusion(bf16[512,3584]{1,0:T(8,128)(2,1)} %bitcast.18, bf16[512,512]{1,0:T(8,128)(2,1)S(1)} %all_gather.14), kind=kOutput, calls=%fused_computation.3 | convolution fusion | flops 1880883200 | bytes 7864320 | tf_op jit(solution)/shard_map/dot_general | solution.py:52
  214.5 5.9 %copy.11 = bf16[512,3584]{1,0:T(8,128)(2,1)} copy(bf16[512,3584]{0,1:T(8,128)(2,1)} %fusion) | data formatting | bytes 7340032
  220.4 6.1 %fusion.1 = bf16[512,3584]{0,1:T(8,128)(2,1)} fusion(bf16[512,3584]{1,0:T(8,128)(2,1)} %all-gather.3.cloned.1.call-done, bf16[512,512]{1,0:T(8,128)(2,1)S(1)} %all_gather.14), kind=kOutput, calls=%fused_computation.4 | convolution fusion | flops 1880883200 | bytes 7864320 | tf_op jit(solution)/shard_map/dot_general | solution.py:55
  226.5 5.9 %copy.12 = bf16[512,3584]{1,0:T(8,128)(2,1)} copy(bf16[512,3584]{0,1:T(8,128)(2,1)} %fusion.1) | data formatting | bytes 7340032
  232.4 7.2 %all-gather.5.cloned.1.call-done = bf16[512,3584]{1,0:T(8,128)(2,1)} async-done(((bf16[32,3584]{1,0:T(8,128)(2,1)}), bf16[512,3584]{1,0:T(8,128)(2,1)}) %all-gather.5.cloned.1.call-update) | async-done | bytes 3670032 | tf_op jit(solution)/shard_map/all_gather | solution.py:45
  239.6 6.0 %convolution_convert_fusion = bf16[3584,512]{1,0:T(8,128)(2,1)} fusion(bf16[512,3584]{1,0:T(8,128)(2,1)} %all-gather.5.cloned.1.call-done, bf16[512,512]{1,0:T(8,128)(2,1)S(1)} %all_gather.12), kind=kOutput, calls=%fused_computation | convolution fusion | flops 1880883200 | bytes 7864320 | tf_op jit(solution)/shard_map/dot_general | solution.py:49
  245.6 27.7 %reduce-scatter.5.cloned.1.call-done = f32[64,512]{1,0:T(8,128)} async-done(((f32[512,512]{1,0:T(8,128)}), f32[64,512]{1,0:T(8,128)}) %reduce-scatter.5.cloned.1.call-update) | async-done | bytes 131088 | tf_op jit(solution)/shard_map/reduce_scatter | solution.py:59
  273.3 1.5 convert_element_type.37
Async XLA Ops:
  7.2 106.1 %reduce-scatter.3.cloned.1.call-start = ((), (), s32[]{:S(2)}) async-start(), calls=%async_computation.3 | async-start | bytes 7798784 | tf_op jit(solution)/shard_map/reduce_scatter | solution.py:37
  28.9 84.4 %copy-start.1 = (bf16[32,3584]{1,0:T(8,128)(2,1)S(1)}, bf16[32,3584]{1,0:T(8,128)(2,1)}, u32[]{:S(2)}) copy-start(bf16[32,3584]{1,0:T(8,128)(2,1)} %param.9) | copy-start | bytes 688132
  28.9 84.4 %copy-start.2 = (bf16[32,3584]{1,0:T(8,128)(2,1)S(1)}, bf16[32,3584]{1,0:T(8,128)(2,1)}, u32[]{:S(2)}) copy-start(bf16[32,3584]{1,0:T(8,128)(2,1)} %param.10) | copy-start | bytes 688132
  28.9 159.5 %all-gather.3.cloned.1.call-start = ((), (), s32[]{:S(2)}) async-start(), calls=%async_computation.4 | async-start | bytes 3899392 | tf_op jit(solution)/shard_map/all_gather | solution.py:47
  115.4 124.2 %all-gather.5.cloned.1.call-start = ((), (), s32[]{:S(2)}) async-start(), calls=%async_computation.6 | async-start | bytes 3899392 | tf_op jit(solution)/shard_map/all_gather | solution.py:45
  116.1 157.2 %reduce-scatter.5.cloned.1.call-start = ((), (), s32[]{:S(2)}) async-start(), calls=%async_computation.5 | async-start | bytes 1179648 | tf_op jit(solution)/shard_map/reduce_scatter | solution.py:59
  116.5 55.6 %copy-start.4 = (bf16[512,3584]{1,0:T(8,128)(2,1)S(1)}, bf16[512,3584]{1,0:T(8,128)(2,1)}, u32[]{:S(2)}) copy-start(bf16[512,3584]{1,0:T(8,128)(2,1)} %param.11) | copy-start | bytes 11010052
  170.3 1.8 copy-start
  174.2 20.5 %copy-start.3 = (bf16[64,512]{1,0:T(8,128)(2,1)S(1)}, bf16[64,512]{1,0:T(8,128)(2,1)}, u32[]{:S(2)}) copy-start(bf16[64,512]{1,0:T(8,128)(2,1)} %param.7) | copy-start | bytes 196612
Sparse Core Ops, SparseCore 0:
  29.1 84.2 reduce-scatter.2
  116.2 72.1 all-gather.2
  190.8 48.7 all-gather.4
  242.0 31.2 reduce-scatter.4
